TPU v7x, 128 devices: a whole 4x4x4 slice. The times are simulated.
128 devices in a mesh: tmpl: 16 (over x, y), sta: 8 (over z, core).
Axes of the slice: x: 4, y: 4, z: 4, core: 2. Of those that a mesh axis runs over, the one named last changes fastest.
Arguments:
- waveforms: bfloat16 [6144, 9088], P(('tmpl', 'sta'))
- template_taps: bfloat16 [24576, 400], P(('tmpl', 'sta')), may hold values from -6 to 6
- slot_template: int32 [24576], P(('tmpl', 'sta')), may hold values from 0 to 127
- slot_channel: int32 [24576], P(('tmpl', 'sta')), may hold values from 0 to 6143, as said below
- slot_moveout: int32 [24576], P(('tmpl', 'sta')), may hold values from 0 to 383
Outputs:
- stacks: float32 [8192, 2048], P('sta', 'tmpl')
Inputs may be any that keep to these rules, and one draw needn't show every extreme that they name: Entry s lies in the station group of its aligned block b = s // 192 of entries: (slot_channel[s] // 48) % 8 equals b % 8. Within one aligned block, the entries take at most 8 distinct channels from any one block of 48 channels (c // 48 equal), and in every aligned block some block of channels gives exactly 8.
All inputs are finite; a program needn't handle non-finite values.
Results may differ from a plain program's by a relative error of at most 0.0029.
Values may be sent and summed in bfloat16 or wider, within the bound.
A program may use at most 128 MiB of HBM per device.

v0:
```python
import math

import jax
import jax.numpy as jnp
from jax import lax
from jax.sharding import PartitionSpec as P

TAPS = 400
CH_TPL = 30
LAGS = 8192
TPL_DEV = 128
CAP = 8


def toeplitz(tap_rows, span_blocks):
    span_width = span_blocks * 128
    padded = jnp.concatenate(
        [
            tap_rows,
            jnp.zeros((tap_rows.shape[0], span_width + 1 - tap_rows.shape[1]), tap_rows.dtype),
        ],
        axis=1,
    )
    tiled = jnp.tile(padded, (1, 128))[:, : 128 * span_width]
    return tiled.reshape(tap_rows.shape[0], 128, span_width)


def plan_rows(channel_block, channels_here, owners, groups):
    owner_ids = channel_block // channels_here // groups
    local_ids = channel_block % channels_here
    keyed = owner_ids * channels_here + local_ids
    onehot = keyed[:, None] == jnp.arange(owners * channels_here, dtype=jnp.int32)[None, :]
    needed = jnp.any(onehot, axis=0).reshape(owners, channels_here)
    ranks = jnp.cumsum(needed.astype(jnp.int32), axis=1) - 1
    picks = needed[:, :, None] & (
        ranks[:, :, None] == jnp.arange(CAP, dtype=jnp.int32)[None, None, :]
    )
    request = jnp.sum(
        jnp.where(picks, jnp.arange(channels_here, dtype=jnp.int32)[None, :, None], 0), axis=1
    )
    slot_rank = jnp.sum(jnp.where(onehot, ranks.reshape(-1)[None, :], 0), axis=1)
    return (request, owner_ids, keyed, slot_rank)


def correlate_stack(source_rows, row_ids, moveouts_all, taps_all, templates_all, lags_here):
    eps = 1e-06
    span_blocks = (TAPS + 127) // 128 + 1
    wide_blocks = span_blocks + 1
    wide_width = wide_blocks * 128
    lag_blocks = lags_here // 128
    source_blocks = source_rows.shape[1] // 128
    table = source_rows.reshape(-1, 128)
    scale = math.sqrt(TAPS / CH_TPL)
    labels = (templates_all[:, None] == jnp.arange(TPL_DEV, dtype=jnp.int32)[None, :]).astype(
        jnp.bfloat16
    )
    per_block = min(32, row_ids.shape[0])
    scan_inputs = (
        row_ids.reshape(-1, per_block),
        moveouts_all.reshape(-1, per_block),
        taps_all.reshape(-1, per_block, TAPS),
        labels.reshape(-1, per_block, TPL_DEV),
    )
    columns = jnp.arange(wide_width, dtype=jnp.int32)
    tap_index = jnp.arange(TAPS, dtype=jnp.int32)
    lagged = jnp.arange(128, dtype=jnp.int32)
    block_steps = jnp.arange(lag_blocks + span_blocks, dtype=jnp.int32)

    def one_block(stack, pieces):
        block_rows, moveouts, tap_rows, label_rows = pieces
        coarse = moveouts // 128
        offset_fine = moveouts % 128
        block_index = (block_rows * source_blocks + coarse)[:, None] + block_steps[None, :]
        segment = table[block_index]
        segment_float = segment.astype(jnp.float32)
        squares = (segment_float * segment_float).astype(jnp.bfloat16)
        framed = jnp.concatenate(
            [segment[:, offset : offset + lag_blocks] for offset in range(wide_blocks)], axis=-1
        )
        framed_sq = jnp.concatenate(
            [squares[:, offset : offset + lag_blocks] for offset in range(wide_blocks)], axis=-1
        )
        placer = (
            columns[None, None, :] == tap_index[None, :, None] + offset_fine[:, None, None]
        ).astype(jnp.bfloat16)
        placed = jnp.einsum(
            "bk,bku->bu", tap_rows, placer, preferred_element_type=jnp.float32
        ).astype(jnp.bfloat16)
        corr = jnp.einsum(
            "bqu,bru->bqr",
            framed,
            toeplitz(placed, wide_blocks),
            preferred_element_type=jnp.float32,
        )
        start_col = lagged[None, None, :] + offset_fine[:, None, None]
        band = (
            (columns[None, :, None] >= start_col) & (columns[None, :, None] < start_col + TAPS)
        ).astype(jnp.bfloat16)
        energy = jnp.einsum("bqu,bur->bqr", framed_sq, band, preferred_element_type=jnp.float32)
        taps_float = tap_rows.astype(jnp.float32)
        tap_energy = jnp.sum(taps_float * taps_float, axis=1)
        normed = scale * corr * lax.rsqrt(tap_energy + eps)[:, None, None] * lax.rsqrt(energy + eps)
        normed = normed.astype(jnp.bfloat16).reshape(per_block, lags_here)
        stack = stack + lax.dot_general(
            normed, label_rows, (((0,), (0,)), ((), ())), preferred_element_type=jnp.float32
        )
        return (stack, None)

    initial = jnp.zeros((lags_here, TPL_DEV), jnp.float32)
    stack, leftover = lax.scan(one_block, initial, scan_inputs)
    return stack


def per_device(waveforms, template_taps, slot_template, slot_channel, slot_moveout):
    groups = lax.axis_size("sta")
    owners = lax.axis_size("tmpl")
    channels_here = waveforms.shape[0]
    request, owner_ids, keyed, slot_rank = plan_rows(slot_channel, channels_here, owners, groups)
    source_rows = lax.all_gather(waveforms, "tmpl", axis=0, tiled=True)
    stack = correlate_stack(source_rows, keyed, slot_moveout, template_taps, slot_template, LAGS)
    return lax.psum_scatter(stack, "sta", scatter_dimension=0, tiled=True)


def solution(mesh):
    return jax.shard_map(
        per_device,
        mesh=mesh,
        in_specs=(
            P(("tmpl", "sta"), None),
            P(("tmpl", "sta"), None),
            P(("tmpl", "sta")),
            P(("tmpl", "sta")),
            P(("tmpl", "sta")),
        ),
        out_specs=P("sta", "tmpl"),
        check_vma=False,
    )
```

profile of v0, /device:TPU:1, one launch (start us, length us, event | category | flops | bytes accessed | tf_op | source)
XLA Modules:
  0.0 548.5 jit_solution(6023225751568051309)
XLA Ops:
  9.7 99.6 %all-gather.2.cloned.1.call-done = bf16[768,9088]{1,0:T(8,128)(2,1)} async-done(((bf16[48,9088]{1,0:T(8,128)(2,1)}), bf16[768,9088]{1,0:T(8,128)(2,1)}) %all-gather.2.cloned.1.call-update) | async-done | bytes 13959184 | tf_op jit(solution)/shard_map/all_gather | solution.py:119
  109.3 28.3 %reshape.246 = bf16[54528,128]{1,0:T(8,128)(2,1)} reshape(bf16[768,9088]{1,0:T(8,128)(2,1)} %all-gather.2.cloned.1.call-done) | data formatting | bytes 27918336 | tf_op jit(solution)/shard_map/reshape | solution.py:52
  137.5 368.7 %while.14 = (s32[]{:T(128)}, f32[8192,128]{1,0:T(8,128)}, s32[6,32]{1,0:T(8,128)S(1)}, s32[6,32]{1,0:T(8,128)S(1)}, bf16[54528,128]{1,0:T(8,128)(2,1)}, /*index=...) while((s32[]{:T(128)}, f32[8192,128]{1,0:T(8,128)}, ...), condition=%wide.region_2.3_spmd.clone.clone, body=%wide.region_0.2_spmd.clone.clone.sunk | while | flops 915409344 | bytes 91079840 | solution.py:110
  137.8 10.9 %gather_fusion = bf16[2208,128]{1,0:T(8,128)(2,1)S(1)} fusion(bf16[54528,128]{1,0:T(8,128)(2,1)} %get-tuple-element.304, s32[3072]{0:T(1024)S(1)} %pad_clamp_fusion.2), kind=kCustom, calls=%fused_computation.clone.clone.1 | custom fusion | bytes 1139328 | tf_op jit(solution)/shard_map/while/body/eval_jaxpr/gather | solution.py:74
  161.2 8.1 %fusion.58 = bf16[32,1,768]{2,1,0:T(2,128)(2,1)S(1)} fusion(s32[32,400]{1,0:T(8,128)S(1)} %iota_add_fusion.6, bf16[32,400,1]{1,0,2:T(8,128)(2,1)S(1)} %dynamic-slice_bitcast_fusion.2), kind=kOutput, calls=%fused_computation.6.clone.1 | convolution fusion | flops 29491200 | bytes 125952 | tf_op jit(solution)/shard_map/while/body/eval_jaxpr/bk,bku->bu/dot_general | solution.py:86
  172.8 12.2 %tile.19 = bf16[32,98432]{1,0:T(8,128)(2,1)} reshape(bf16[32,128,769]{2,1,0:T(8,128)(2,1)} %tile.18) | data formatting | bytes 12599296 | tf_op jit(solution)/shard_map/while/body/eval_jaxpr/tile | solution.py:24
  190.2 4.2 fusion.59
  197.4 10.9 %gather_fusion = bf16[2208,128]{1,0:T(8,128)(2,1)S(1)} fusion(bf16[54528,128]{1,0:T(8,128)(2,1)} %get-tuple-element.304, s32[3072]{0:T(1024)S(1)} %pad_clamp_fusion.2), kind=kCustom, calls=%fused_computation.clone.clone.1 | custom fusion | bytes 1139328 | tf_op jit(solution)/shard_map/while/body/eval_jaxpr/gather | solution.py:74
  220.8 8.1 %fusion.58 = bf16[32,1,768]{2,1,0:T(2,128)(2,1)S(1)} fusion(s32[32,400]{1,0:T(8,128)S(1)} %iota_add_fusion.6, bf16[32,400,1]{1,0,2:T(8,128)(2,1)S(1)} %dynamic-slice_bitcast_fusion.2), kind=kOutput, calls=%fused_computation.6.clone.1 | convolution fusion | flops 29491200 | bytes 125952 | tf_op jit(solution)/shard_map/while/body/eval_jaxpr/bk,bku->bu/dot_general | solution.py:86
  232.5 12.2 %tile.19 = bf16[32,98432]{1,0:T(8,128)(2,1)} reshape(bf16[32,128,769]{2,1,0:T(8,128)(2,1)} %tile.18) | data formatting | bytes 12599296 | tf_op jit(solution)/shard_map/while/body/eval_jaxpr/tile | solution.py:24
  254.0 4.9 convolution_add_fusion.2
  259.2 10.9 %gather_fusion = bf16[2208,128]{1,0:T(8,128)(2,1)S(1)} fusion(bf16[54528,128]{1,0:T(8,128)(2,1)} %get-tuple-element.304, s32[3072]{0:T(1024)S(1)} %pad_clamp_fusion.2), kind=kCustom, calls=%fused_computation.clone.clone.1 | custom fusion | bytes 1139328 | tf_op jit(solution)/shard_map/while/body/eval_jaxpr/gather | solution.py:74
  282.6 8.1 %fusion.58 = bf16[32,1,768]{2,1,0:T(2,128)(2,1)S(1)} fusion(s32[32,400]{1,0:T(8,128)S(1)} %iota_add_fusion.6, bf16[32,400,1]{1,0,2:T(8,128)(2,1)S(1)} %dynamic-slice_bitcast_fusion.2), kind=kOutput, calls=%fused_computation.6.clone.1 | convolution fusion | flops 29491200 | bytes 125952 | tf_op jit(solution)/shard_map/while/body/eval_jaxpr/bk,bku->bu/dot_general | solution.py:86
  294.3 12.2 %tile.19 = bf16[32,98432]{1,0:T(8,128)(2,1)} reshape(bf16[32,128,769]{2,1,0:T(8,128)(2,1)} %tile.18) | data formatting | bytes 12599296 | tf_op jit(solution)/shard_map/while/body/eval_jaxpr/tile | solution.py:24
  311.7 4.2 fusion.59
  315.9 4.9 convolution_add_fusion.2
  321.0 10.9 %gather_fusion = bf16[2208,128]{1,0:T(8,128)(2,1)S(1)} fusion(bf16[54528,128]{1,0:T(8,128)(2,1)} %get-tuple-element.304, s32[3072]{0:T(1024)S(1)} %pad_clamp_fusion.2), kind=kCustom, calls=%fused_computation.clone.clone.1 | custom fusion | bytes 1139328 | tf_op jit(solution)/shard_map/while/body/eval_jaxpr/gather | solution.py:74
  344.4 8.1 %fusion.58 = bf16[32,1,768]{2,1,0:T(2,128)(2,1)S(1)} fusion(s32[32,400]{1,0:T(8,128)S(1)} %iota_add_fusion.6, bf16[32,400,1]{1,0,2:T(8,128)(2,1)S(1)} %dynamic-slice_bitcast_fusion.2), kind=kOutput, calls=%fused_computation.6.clone.1 | convolution fusion | flops 29491200 | bytes 125952 | tf_op jit(solution)/shard_map/while/body/eval_jaxpr/bk,bku->bu/dot_general | solution.py:86
  356.1 12.2 %tile.19 = bf16[32,98432]{1,0:T(8,128)(2,1)} reshape(bf16[32,128,769]{2,1,0:T(8,128)(2,1)} %tile.18) | data formatting | bytes 12599296 | tf_op jit(solution)/shard_map/while/body/eval_jaxpr/tile | solution.py:24
  373.5 4.2 fusion.59
  377.7 4.9 convolution_add_fusion.2
  382.9 10.9 %gather_fusion = bf16[2208,128]{1,0:T(8,128)(2,1)S(1)} fusion(bf16[54528,128]{1,0:T(8,128)(2,1)} %get-tuple-element.304, s32[3072]{0:T(1024)S(1)} %pad_clamp_fusion.2), kind=kCustom, calls=%fused_computation.clone.clone.1 | custom fusion | bytes 1139328 | tf_op jit(solution)/shard_map/while/body/eval_jaxpr/gather | solution.py:74
  406.2 8.1 %fusion.58 = bf16[32,1,768]{2,1,0:T(2,128)(2,1)S(1)} fusion(s32[32,400]{1,0:T(8,128)S(1)} %iota_add_fusion.6, bf16[32,400,1]{1,0,2:T(8,128)(2,1)S(1)} %dynamic-slice_bitcast_fusion.2), kind=kOutput, calls=%fused_computation.6.clone.1 | convolution fusion | flops 29491200 | bytes 125952 | tf_op jit(solution)/shard_map/while/body/eval_jaxpr/bk,bku->bu/dot_general | solution.py:86
  417.9 12.2 %tile.19 = bf16[32,98432]{1,0:T(8,128)(2,1)} reshape(bf16[32,128,769]{2,1,0:T(8,128)(2,1)} %tile.18) | data formatting | bytes 12599296 | tf_op jit(solution)/shard_map/while/body/eval_jaxpr/tile | solution.py:24
  435.3 4.2 fusion.59
  439.5 4.9 convolution_add_fusion.2
  444.7 10.9 %gather_fusion = bf16[2208,128]{1,0:T(8,128)(2,1)S(1)} fusion(bf16[54528,128]{1,0:T(8,128)(2,1)} %get-tuple-element.304, s32[3072]{0:T(1024)S(1)} %pad_clamp_fusion.2), kind=kCustom, calls=%fused_computation.clone.clone.1 | custom fusion | bytes 1139328 | tf_op jit(solution)/shard_map/while/body/eval_jaxpr/gather | solution.py:74
  468.1 8.1 %fusion.58 = bf16[32,1,768]{2,1,0:T(2,128)(2,1)S(1)} fusion(s32[32,400]{1,0:T(8,128)S(1)} %iota_add_fusion.6, bf16[32,400,1]{1,0,2:T(8,128)(2,1)S(1)} %dynamic-slice_bitcast_fusion.2), kind=kOutput, calls=%fused_computation.6.clone.1 | convolution fusion | flops 29491200 | bytes 125952 | tf_op jit(solution)/shard_map/while/body/eval_jaxpr/bk,bku->bu/dot_general | solution.py:86
  479.7 12.2 %tile.19 = bf16[32,98432]{1,0:T(8,128)(2,1)} reshape(bf16[32,128,769]{2,1,0:T(8,128)(2,1)} %tile.18) | data formatting | bytes 12599296 | tf_op jit(solution)/shard_map/while/body/eval_jaxpr/tile | solution.py:24
  497.1 4.2 fusion.59
  501.3 4.9 convolution_add_fusion.2
  506.3 35.3 %reduce-scatter.2.cloned.1.call-done = f32[1024,128]{1,0:T(8,128)} async-done(((f32[8192,128]{1,0:T(8,128)}), f32[1024,128]{1,0:T(8,128)}) %reduce-scatter.2.cloned.1.call-update) | async-done | bytes 524304 | tf_op jit(solution)/shard_map/reduce_scatter | solution.py:121
  (198 shorter events, 137.9 us)
Async XLA Ops:
  6.5 102.7 %all-gather.2.cloned.1.call-start = ((), (), s32[]{:S(2)}) async-start(), calls=%async_computation.1 | async-start | bytes 14831616 | tf_op jit(solution)/shard_map/all_gather | solution.py:119
  7.3 534.4 %reduce-scatter.2.cloned.1.call-start = ((), (), s32[]{:S(2)}) async-start(), calls=%async_computation.2 | async-start | bytes 4718592 | tf_op jit(solution)/shard_map/reduce_scatter | solution.py:121
  185.1 2.8 slice-start
  244.7 2.8 slice-start
  306.5 2.8 slice-start
  368.3 2.8 slice-start
  430.2 2.8 slice-start
  492.0 2.8 slice-start
Sparse Core Ops, SparseCore 0:
  9.5 99.6 all-gather.1
  506.4 35.1 reduce-scatter.1
where the time goes:
time: 553 us; the launch traced here: 548 us
  local copies, waits for them, and re-layouts  266 us (48%)
  waiting for transfers between devices  136 us (25%)
  matrix products  124 us (22%)
  between operations  13.4 us (2%)
  other arithmetic  8.36 us (2%)
    all_gather x1, waiting for transfers between devices, per_device(): source_rows = lax.all_gather(waveforms, 'tmpl', axis=0, tiled=True)  99.6 us
    another operation x12, local copies, waits for them, and re-layouts, toeplitz(): tiled = jnp.tile(padded, (1, 128))[:, :128 * span_width]  94.7 us
    gather x12, local copies, waits for them, and re-layouts, one_block(): segment = table[block_index]  66.6 us
    dot_general x6, matrix products, one_block(): jnp.einsum('bk,bku->bu', tap_rows, placer, preferred_element_type=jnp.flo...  48.6 us
    while x66, local copies, waits for them, and re-layouts  45.2 us
    reduce_scatter x1, waiting for transfers between devices, per_device(): return lax.psum_scatter(stack, 'sta', scatter_dimension=0, tiled=True)  35.3 us
    reshape x1, local copies, waits for them, and re-layouts, correlate_stack(): table = source_rows.reshape(-1, 128)  28.3 us
    dot_general x6, matrix products, one_block(): lax.dot_general(normed, label_rows, (((0,), (0,)), ((), ())), preferred_e...  27.5 us
  transfers between devices with their start and end apart: 2, of which 2 were waited for; matrix products, arithmetic and copies ran while one was open for 0% of the time, Pallas kernels for 0%

commit v1 on v0

v1 whole, which is shorter than its diff:
```python
import functools
import math

import jax
import jax.numpy as jnp
from jax import lax
from jax.experimental import pallas as pl
from jax.experimental.pallas import tpu as pltpu
from jax.sharding import PartitionSpec as P

TAPS = 400
CH_TPL = 30
LAGS = 8192
TPL_DEV = 128
CAP = 8
EPS = 1e-06
SCALE = math.sqrt(TAPS / CH_TPL)
LANES = 128
SPAN = 5
LAG_BLOCKS = LAGS // LANES
ROWS = 72
MESH = pl.DeviceIdType.MESH

OFFSETS = (
    (1, 0), (3, 0), (0, 1), (0, 3), (1, 1), (3, 3), (1, 3), (3, 1),
    (2, 0), (0, 2), (2, 1), (1, 2), (2, 3), (3, 2), (2, 2),
)


def plan_rows(slot_channel, channels_here, owners, groups):
    owner = slot_channel // channels_here // groups
    local = slot_channel % channels_here
    key = owner * channels_here + local
    count = key.shape[0]
    order = jnp.arange(count, dtype=jnp.int32)
    earlier = (key[:, None] == key[None, :]) & (order[None, :] < order[:, None])
    first = ~jnp.any(earlier, axis=1)
    below = (owner[:, None] == owner[None, :]) & (key[None, :] < key[:, None]) & first[None, :]
    row = owner * CAP + jnp.sum(below.astype(jnp.int32), axis=1)
    hit = (row[:, None] == jnp.arange(owners * CAP, dtype=jnp.int32)[None, :]) & first[:, None]
    request = jnp.sum(jnp.where(hit, local[:, None], 0), axis=0)
    return request, row


def fetch_kernel(req_smem, req_ref, wave_ref, out_ref, req_all, send, req_here, req_send, req_recv, data_send, data_recv, local_sem):
    me = lax.axis_index("tmpl")
    x, y = me // 4, me % 4
    peers = [((x + dx) % 4) * 4 + (y + dy) % 4 for dx, dy in OFFSETS]
    sources = [((x + 4 - dx) % 4) * 4 + (y + 4 - dy) % 4 for dx, dy in OFFSETS]
    count = len(peers)

    barrier = pltpu.get_barrier_semaphore()
    for peer in peers:
        pl.semaphore_signal(barrier, inc=1, device_id={"tmpl": peer}, device_id_type=MESH)
    pl.semaphore_wait(barrier, count)

    asks = []
    for d, peer in enumerate(peers):
        copy = pltpu.make_async_remote_copy(
            src_ref=req_ref,
            dst_ref=req_all.at[d],
            send_sem=req_send.at[d],
            recv_sem=req_recv.at[d],
            device_id={"tmpl": peer},
            device_id_type=MESH,
        )
        copy.start()
        asks.append(copy)
    for k in range(CAP):
        out_ref[me * CAP + k] = wave_ref[req_smem[0, me * CAP + k]]
    for copy in asks:
        copy.wait()
    here = pltpu.make_async_copy(req_all, req_here, local_sem)
    here.start()
    here.wait()

    sends = []
    for d in range(count):
        back = OFFSETS.index(((4 - OFFSETS[d][0]) % 4, (4 - OFFSETS[d][1]) % 4))
        for k in range(CAP):
            send[d * CAP + k] = wave_ref[req_here[back, 0, me * CAP + k]]
        copy = pltpu.make_async_remote_copy(
            src_ref=send.at[pl.ds(d * CAP, CAP)],
            dst_ref=out_ref.at[pl.ds(me * CAP, CAP)],
            send_sem=data_send.at[d],
            recv_sem=data_recv.at[d],
            device_id={"tmpl": peers[d]},
            device_id_type=MESH,
        )
        copy.start()
        sends.append(copy)
    for copy in sends:
        copy.wait()


def fetch(request, waves, owners):
    blocks = waves.shape[1] // LANES
    waves = jnp.pad(waves.reshape(waves.shape[0], blocks, LANES), ((0, 0), (0, ROWS - blocks), (0, 0)))
    wide = jnp.broadcast_to(request[None, :], (8, request.shape[0]))
    peers = owners - 1
    return pl.pallas_call(
        fetch_kernel,
        out_shape=jax.ShapeDtypeStruct((owners * CAP, ROWS, LANES), jnp.bfloat16),
        in_specs=[
            pl.BlockSpec(memory_space=pltpu.SMEM),
            pl.BlockSpec(memory_space=pltpu.VMEM),
            pl.BlockSpec(memory_space=pltpu.VMEM),
        ],
        out_specs=pl.BlockSpec(memory_space=pltpu.VMEM),
        scratch_shapes=[
            pltpu.VMEM((peers, 8, LANES), jnp.int32),
            pltpu.VMEM((peers * CAP, ROWS, LANES), jnp.bfloat16),
            pltpu.SMEM((peers, 8, LANES), jnp.int32),
            pltpu.SemaphoreType.DMA((peers,)),
            pltpu.SemaphoreType.DMA((peers,)),
            pltpu.SemaphoreType.DMA((peers,)),
            pltpu.SemaphoreType.DMA((peers,)),
            pltpu.SemaphoreType.DMA,
        ],
        compiler_params=pltpu.CompilerParams(collective_id=0, has_side_effects=True),
        name="fetch",
    )(wide, wide, waves)


def correlate_kernel(row_ref, move_ref, core_ref, wave_ref, taps_ref, label_ref, send_ref, keep_ref, frames, inv, band, flipped, norm, toep0, toep1, wide0, wide1, roll0, roll1, ncc):
    channels = wave_ref.shape[0]
    slots = taps_ref.shape[0]
    sub = lax.broadcasted_iota(jnp.int32, (LANES, LANES), 0)
    lane = lax.broadcasted_iota(jnp.int32, (LANES, LANES), 1)

    column = lax.broadcasted_iota(jnp.int32, (SPAN * LANES, LANES), 0)
    lagged = lax.broadcasted_iota(jnp.int32, (SPAN * LANES, LANES), 1)
    band[...] = jnp.where((column >= lagged) & (column < lagged + TAPS), 1.0, 0.0).astype(jnp.bfloat16)
    flip = jnp.where(sub == (LANES - lane) % LANES, 1.0, 0.0).astype(jnp.bfloat16)
    power = jnp.zeros((slots, 1), jnp.float32)
    for b in range(4):
        piece = taps_ref[:, b * LANES : (b + 1) * LANES]
        flipped[b] = jnp.dot(piece, flip, preferred_element_type=jnp.float32)
        piece = piece.astype(jnp.float32)
        power = power + jnp.sum(piece * piece, axis=1, keepdims=True)
    norm[...] = jnp.broadcast_to(SCALE * lax.rsqrt(power + EPS), (slots, LANES))

    for wide in (wide0, wide1):
        wide[ROWS:, :] = jnp.zeros((8, LANES), jnp.float32)

    def channel_pair(i, carry):
        for p, wide in enumerate((wide0, wide1)):
            c = 2 * i + p
            wide[:ROWS, :] = wave_ref[c].astype(jnp.float32)
            frame = jnp.concatenate([wide[a : a + ROWS, :] for a in range(SPAN)], axis=1)
            frames[c] = frame.astype(jnp.bfloat16)
            squares = (frame * frame).astype(jnp.bfloat16)
            energy = jnp.dot(squares, band[...], preferred_element_type=jnp.float32)
            inv[c] = lax.rsqrt(energy + EPS)
        return carry

    lax.fori_loop(0, channels // 2, channel_pair, 0)

    lower = lane <= sub
    edge = lax.broadcasted_iota(jnp.int32, (LAG_BLOCKS, LANES), 1)

    def slot_pair(i, carry):
        for p, (toep, rolled) in enumerate(((toep0, roll0), (toep1, roll1))):
            s = 2 * i + p
            row = row_ref[s]
            move = move_ref[s]
            coarse = move // LANES
            fine = move % LANES
            last = jnp.zeros((LANES, LANES), jnp.float32)
            for b in range(4):
                circ = jnp.broadcast_to(flipped[b, pl.ds(s, 1), :], (LANES, LANES))
                circ = pltpu.roll(circ, 0, 1, stride=1, stride_axis=0)
                toep[b * LANES : (b + 1) * LANES, :] = jnp.where(lower, circ, last).astype(jnp.bfloat16)
                last = circ
            toep[4 * LANES :, :] = jnp.where(lower, 0.0, last).astype(jnp.bfloat16)
            corr = jnp.dot(frames[row], toep[...], preferred_element_type=jnp.float32)
            normed = corr * jnp.broadcast_to(norm[pl.ds(s, 1), :], corr.shape) * inv[row]
            normed = normed.astype(jnp.bfloat16).astype(jnp.float32)
            rolled[...] = pltpu.roll(normed, (LANES - fine) % LANES, 1)
            near = rolled[pl.ds(coarse, LAG_BLOCKS), :]
            far = rolled[pl.ds(coarse + 1, LAG_BLOCKS), :]
            ncc[pl.ds(s * LAG_BLOCKS, LAG_BLOCKS), :] = jnp.where(edge < LANES - fine, near, far)
        return carry

    lax.fori_loop(0, slots // 2, slot_pair, 0)

    core = core_ref[0]

    def block(i, carry):
        z, q = i // 8, i % 8
        for h in range(2):
            at = (2 * z + (core + h) % 2) * 8 + q
            picked = ncc[pl.ds(at, slots, stride=LAG_BLOCKS), :].astype(jnp.bfloat16)
            total = jnp.dot(label_ref[...], picked, preferred_element_type=jnp.float32)
            if h == 0:
                keep_ref[i] = total
            else:
                send_ref[i] = total.astype(jnp.bfloat16)
        return carry

    lax.fori_loop(0, LAG_BLOCKS // 2, block, 0)


def correlate(rows, moveouts, core, source, taps, templates):
    slots = taps.shape[0]
    channels = source.shape[0]
    taps = jnp.pad(taps, ((0, 0), (0, 4 * LANES - TAPS)))
    label = (jnp.arange(TPL_DEV, dtype=jnp.int32)[:, None] == templates[None, :]).astype(jnp.bfloat16)
    half = LAG_BLOCKS // 2
    vmem = pl.BlockSpec(memory_space=pltpu.VMEM)
    smem = pl.BlockSpec(memory_space=pltpu.SMEM)
    return pl.pallas_call(
        correlate_kernel,
        out_shape=(
            jax.ShapeDtypeStruct((half, TPL_DEV, LANES), jnp.bfloat16),
            jax.ShapeDtypeStruct((half, TPL_DEV, LANES), jnp.float32),
        ),
        in_specs=[smem, smem, smem, vmem, vmem, vmem],
        out_specs=(vmem, vmem),
        scratch_shapes=[
            pltpu.VMEM((channels, ROWS, SPAN * LANES), jnp.bfloat16),
            pltpu.VMEM((channels, ROWS, LANES), jnp.float32),
            pltpu.VMEM((SPAN * LANES, LANES), jnp.bfloat16),
            pltpu.VMEM((4, slots, LANES), jnp.float32),
            pltpu.VMEM((slots, LANES), jnp.float32),
            pltpu.VMEM((SPAN * LANES, LANES), jnp.bfloat16),
            pltpu.VMEM((SPAN * LANES, LANES), jnp.bfloat16),
            pltpu.VMEM((ROWS + 8, LANES), jnp.float32),
            pltpu.VMEM((ROWS + 8, LANES), jnp.float32),
            pltpu.VMEM((ROWS, LANES), jnp.float32),
            pltpu.VMEM((ROWS, LANES), jnp.float32),
            pltpu.VMEM((slots * LAG_BLOCKS, LANES), jnp.float32),
        ],
        compiler_params=pltpu.CompilerParams(vmem_limit_bytes=56 << 20),
        name="correlate",
    )(rows, moveouts, core, source, taps, label)


def combine_kernel(send_ref, keep_ref, out_ref, near, far, outgoing, near_send, near_recv, far_send, far_recv):
    me = lax.axis_index("sta")
    z, core = me // 2, me % 2
    partner = z * 2 + (core + 1) % 2
    others = [(z + step) % 4 for step in (2, 1, 3)]

    barrier = pltpu.get_barrier_semaphore()
    for peer in [partner] + [other * 2 + core for other in others]:
        pl.semaphore_signal(barrier, inc=1, device_id={"sta": peer}, device_id_type=MESH)
    pl.semaphore_wait(barrier, 4)

    firsts = []
    for n, other in enumerate(others + [z]):
        copy = pltpu.make_async_remote_copy(
            src_ref=send_ref.at[pl.ds(other * 8, 8)],
            dst_ref=near.at[n],
            send_sem=near_send.at[n],
            recv_sem=near_recv.at[n],
            device_id={"sta": partner},
            device_id_type=MESH,
        )
        copy.start()
        firsts.append(copy)
    seconds = []
    for n, other in enumerate(others):
        firsts[n].wait()
        for q in range(8):
            outgoing[n, q] = (keep_ref[other * 8 + q] + near[n, q].astype(jnp.float32)).astype(jnp.bfloat16)
        copy = pltpu.make_async_remote_copy(
            src_ref=outgoing.at[n],
            dst_ref=far.at[n],
            send_sem=far_send.at[n],
            recv_sem=far_recv.at[n],
            device_id={"sta": other * 2 + core},
            device_id_type=MESH,
        )
        copy.start()
        seconds.append(copy)
    firsts[3].wait()
    for copy in seconds:
        copy.wait()
    for q in range(8):
        total = keep_ref[z * 8 + q] + near[3, q].astype(jnp.float32)
        for n in range(3):
            total = total + far[n, q].astype(jnp.float32)
        out_ref[q * LANES : (q + 1) * LANES, :] = total.T


def combine(send, keep):
    vmem = pl.BlockSpec(memory_space=pltpu.VMEM)
    return pl.pallas_call(
        combine_kernel,
        out_shape=jax.ShapeDtypeStruct((8 * LANES, TPL_DEV), jnp.float32),
        in_specs=[vmem, vmem],
        out_specs=vmem,
        scratch_shapes=[
            pltpu.VMEM((4, 8, TPL_DEV, LANES), jnp.bfloat16),
            pltpu.VMEM((3, 8, TPL_DEV, LANES), jnp.bfloat16),
            pltpu.VMEM((3, 8, TPL_DEV, LANES), jnp.bfloat16),
            pltpu.SemaphoreType.DMA((4,)),
            pltpu.SemaphoreType.DMA((4,)),
            pltpu.SemaphoreType.DMA((3,)),
            pltpu.SemaphoreType.DMA((3,)),
        ],
        compiler_params=pltpu.CompilerParams(collective_id=1, has_side_effects=True),
        name="combine",
    )(send, keep)


def per_device(waveforms, template_taps, slot_template, slot_channel, slot_moveout):
    groups = lax.axis_size("sta")
    owners = lax.axis_size("tmpl")
    request, rows = plan_rows(slot_channel, waveforms.shape[0], owners, groups)
    source = fetch(request, waveforms, owners)
    core = (lax.axis_index("sta") % 2).astype(jnp.int32).reshape(1)
    send, keep = correlate(rows, slot_moveout, core, source, template_taps, slot_template)
    return combine(send, keep)


def solution(mesh):
    return jax.shard_map(
        per_device,
        mesh=mesh,
        in_specs=(
            P(("tmpl", "sta"), None),
            P(("tmpl", "sta"), None),
            P(("tmpl", "sta")),
            P(("tmpl", "sta")),
            P(("tmpl", "sta")),
        ),
        out_specs=P("sta", "tmpl"),
        check_vma=False,
    )
```

time: 553 us -> 145 us (0.26)
  local copies, waits for them, and re-layouts: 266 us -> 6.7 us
  waiting for transfers between devices: 136 us -> 0 us
  Pallas kernels: 0 us -> 135 us
  matrix products: 124 us -> 0 us
  between operations: 13.4 us -> 0.05 us
  other arithmetic: 8.36 us -> 2.6 us
    pallas_call x0 -> x3, Pallas kernels: none -> 135 us  [the longest x1 69.3 us: correlate(): pl.pallas_call(correlate_kernel, out_shape=(jax.ShapeDtypeStruct((half, T...]
    dot_general x24 -> x0, matrix products: 124 us -> none  [the longest x6 48.6 us: one_block(): jnp.einsum('bk,bku->bu', tap_rows, placer, preferred_element_type=jnp.flo...]
    all_gather x1 -> x0, waiting for transfers between devices: 99.6 us -> none  [per_device(): source_rows = lax.all_gather(waveforms, 'tmpl', axis=0, tiled=True)]
    another operation x12 -> x0, local copies, waits for them, and re-layouts: 94.7 us -> none  [toeplitz(): tiled = jnp.tile(padded, (1, 128))[:, :128 * span_width]]
    gather x12 -> x0, local copies, waits for them, and re-layouts: 66.6 us -> none  [one_block(): segment = table[block_index]]
    while x66 -> x0, local copies, waits for them, and re-layouts: 45.2 us -> none
    reduce_scatter x1 -> x0, waiting for transfers between devices: 35.3 us -> none  [per_device(): return lax.psum_scatter(stack, 'sta', scatter_dimension=0, tiled=True)]
    reshape x3 -> x1, local copies, waits for them, and re-layouts: 29.1 us -> 1.61 us  [fetch(): waves.reshape(waves.shape[0], blocks, LANES)]
  transfers between devices with their start and end apart: 2 -> 0, of which waited for: 2 -> 0; matrix products, arithmetic and copies ran while one was open for 0% -> 0% of each run, Pallas kernels for 0% -> 0%
where the time goes in v1:
time: 145 us; the launch traced here: 144 us
  Pallas kernels  135 us (93%)
  local copies, waits for them, and re-layouts  6.7 us (5%)
  other arithmetic  2.6 us (2%)
    pallas_call x1, Pallas kernels, correlate(): pl.pallas_call(correlate_kernel, out_shape=(jax.ShapeDtypeStruct((half, T...  69.3 us
    pallas_call x1, Pallas kernels, fetch(): pl.pallas_call(fetch_kernel, out_shape=jax.ShapeDtypeStruct((owners * CAP...  42.1 us
    pallas_call x1, Pallas kernels, combine(): pl.pallas_call(combine_kernel, out_shape=jax.ShapeDtypeStruct((8 * LANES,...  23.7 us

profile of v1, /device:TPU:1, one launch (start us, length us, event | category | flops | bytes accessed | tf_op | source)
XLA Modules:
  0.0 144.4 jit_solution(15458278612446505199)
XLA Ops:
  0.0 0.7 multiply_add_fusion
  0.7 0.2 fusion.1
  0.9 0.2 convert_reduce_fusion
  1.1 0.0 copy-start
  1.1 0.2 select_reduce_fusion
  1.3 0.6 broadcast_in_dim.12.req_smem.req_ref
  1.9 1.3 fusion.2.label_ref
  3.2 1.6 %pad.9.taps_ref = bf16[192,512]{1,0:T(8,128)(2,1)} pad(bf16[192,400]{1,0:T(8,128)(2,1)} %param.6, bf16[]{:T(256)} %constant.53.clone.1), padding=0_0x0_112 | pad | bytes 350210 | tf_op jit(solution)/shard_map/jit(_pad)/pad | solution.py:207
  4.8 1.6 %reshape.21 = bf16[48,71,128]{2,1,0:T(8,128)(2,1)S(1)} reshape(bf16[48,9088]{1,0:T(8,128)(2,1)} %param.5) | data formatting | bytes 1744896 | tf_op jit(solution)/shard_map/reshape | solution.py:98
  6.5 1.0 pad.8.wave_ref
  7.5 42.1 %fetch.1.wave_ref = bf16[128,72,128]{2,1,0:T(8,128)(2,1)} custom-call(s32[8,128]{1,0:T(8,128)} %broadcast_in_dim.12.req_smem.req_ref, s32[8,128]{1,0:T(8,128)} %broadcast_in_dim.12.req_smem.req_ref, bf16[48,72,128]{2,1,0:T(8,128)(2,1)} %pad.8.wave_ref), custom_call_target="tpu_custom_call" | custom-call | tf_op jit(solution)/shard_map/fetch/pallas_call | solution.py:101
  49.5 0.0 copy-done
  49.5 69.3 %correlate.1 = (bf16[32,128,128]{2,1,0:T(8,128)(2,1)}, f32[32,128,128]{2,1,0:T(8,128)}) custom-call(s32[192]{0:T(256)} %copy-done, s32[192]{0:T(256)} %move_ref.1, s32[1]{0:T(128)} %bitcast.core_ref, bf16[128,72,128]{2,1,0:T(8,128)(2,1)} %fetch.1.wave_ref, bf16[192,512]{1,0:T(8,128)(2,1)} %pad.9.taps_ref, bf16[128,192]{1,0:T(8,128)(2,1)} %fusion.2.label_ref), custom_call_target="tpu_custom_call" | custom-call | tf_op jit(solution)/shard_map/correlate/pallas_call | solution.py:212
  118.9 23.7 %combine.1 = f32[1024,128]{1,0:T(8,128)} custom-call(bf16[32,128,128]{2,1,0:T(8,128)(2,1)} %get-tuple-element.7.send_ref, f32[32,128,128]{2,1,0:T(8,128)} %get-tuple-element.8.keep_ref), custom_call_target="tpu_custom_call" | custom-call | tf_op jit(solution)/shard_map/combine/pallas_call | solution.py:289
  142.6 1.9 %copy.7 = f32[1024,128]{1,0:T(8,128)} copy(f32[1024,128]{1,0:T(8,128)} %combine.1) | data formatting | bytes 1048576
  (2 shorter events, 0.0 us)
Async XLA Ops:
  1.1 48.4 %copy-start = (s32[192]{0:T(256)}, s32[192]{0:T(256)S(1)}, u32[]{:S(2)}) copy-start(s32[192]{0:T(256)S(1)} %multiply_add_fusion.1.row_ref) | copy-start | bytes 2308

commit v2 on v0

v2 whole, which is shorter than its diff:
```python
import functools
import math

import jax
import jax.numpy as jnp
from jax import lax
from jax.experimental import pallas as pl
from jax.experimental.pallas import tpu as pltpu
from jax.sharding import PartitionSpec as P

TAPS = 400
CH_TPL = 30
LAGS = 8192
TPL_DEV = 128
CAP = 8
EPS = 1e-06
SCALE = math.sqrt(TAPS / CH_TPL)
LANES = 128
SPAN = 5
DEPTH = 528
LAG_BLOCKS = LAGS // LANES
BLOCKS = 71
ROWS = 72
PITCH = LAG_BLOCKS + 1
EARLY = 32
MESH = pl.DeviceIdType.MESH


def plan_rows(slot_channel, channels_here, owners, groups):
    owner = slot_channel // channels_here // groups
    local = slot_channel % channels_here
    key = owner * channels_here + local
    count = key.shape[0]
    order = jnp.arange(count, dtype=jnp.int32)
    earlier = (key[:, None] == key[None, :]) & (order[None, :] < order[:, None])
    first = ~jnp.any(earlier, axis=1)
    below = (owner[:, None] == owner[None, :]) & (key[None, :] < key[:, None]) & first[None, :]
    row = owner * CAP + jnp.sum(below.astype(jnp.int32), axis=1)
    hit = (row[:, None] == jnp.arange(owners * CAP, dtype=jnp.int32)[None, :]) & first[:, None]
    request = jnp.sum(jnp.where(hit, local[:, None], 0), axis=0)
    return request, row


def stack_kernel(
    req_smem, row_ref, move_ref, req_ref, wave_ref, taps_ref, tmpl_ref, out_ref,
    req_all, send, recv, wave32, inv, band, flipped, norm, toep, squares, roll0, roll1, roll2, roll3, ncc, label,
    near_out, near, far_out, far, keep, req_here,
    req_send, req_recv, data_send, data_recv, near_send, near_recv, far_send, far_recv, local_sem,
):
    slots = taps_ref.shape[0]
    me = lax.axis_index("tmpl")
    x, y = me // 4, me % 4
    group = lax.axis_index("sta")
    z, core = group // 2, group % 2
    partner = z * 2 + (core + 1) % 2
    steps = (2, 1, 3)
    count = 16

    def peer(d):
        return ((x + d // 4) % 4) * 4 + (y + d % 4) % 4

    def source(d):
        return ((x + 4 - d // 4) % 4) * 4 + (y + 4 - d % 4) % 4

    barrier = pltpu.get_barrier_semaphore()
    for d in range(1, count):
        pl.semaphore_signal(barrier, inc=1, device_id={"tmpl": peer(d)}, device_id_type=MESH)
    for other in [partner] + [((z + step) % 4) * 2 + core for step in steps]:
        pl.semaphore_signal(barrier, inc=1, device_id={"sta": other}, device_id_type=MESH)

    sub = lax.broadcasted_iota(jnp.int32, (LANES, LANES), 0)
    lane = lax.broadcasted_iota(jnp.int32, (LANES, LANES), 1)
    flip = jnp.where(sub == (LANES - lane) % LANES, 1.0, 0.0).astype(jnp.bfloat16)
    power = jnp.zeros((slots, 1), jnp.float32)
    for b in range(4):
        piece = taps_ref[:, b * LANES : min(b * LANES + LANES, TAPS)]
        wide = piece.shape[1]
        flipped[b] = jnp.dot(piece, flip[:wide, :], preferred_element_type=jnp.float32)
        piece = piece.astype(jnp.float32)
        power = power + jnp.sum(piece * piece, axis=1, keepdims=True)
    norm[...] = jnp.broadcast_to(SCALE * lax.rsqrt(power + EPS), (slots, LANES))
    pl.semaphore_wait(barrier, count - 1 + 4)

    def ask(d):
        return pltpu.make_async_remote_copy(
            src_ref=req_ref,
            dst_ref=req_all.at[d],
            send_sem=req_send.at[d],
            recv_sem=req_recv.at[d],
            device_id={"tmpl": peer(d)},
            device_id_type=MESH,
        )

    for d in range(1, count):
        ask(d).start()

    lower = lane <= sub

    def build(s):
        last = jnp.zeros((LANES, LANES), jnp.float32)
        for b in range(4):
            circ = jnp.broadcast_to(flipped[b, pl.ds(s, 1), :], (LANES, LANES))
            circ = pltpu.roll(circ, 0, 1, stride=1, stride_axis=0)
            toep[s, b * LANES : (b + 1) * LANES, :] = jnp.where(lower, circ, last).astype(jnp.bfloat16)
            last = circ
        tail = DEPTH - 4 * LANES
        toep[s, 4 * LANES :, :] = jnp.where(lower[:tail], 0.0, last[:tail]).astype(jnp.bfloat16)

    def build_pair(i, carry):
        build(2 * i)
        build(2 * i + 1)
        return carry

    lax.fori_loop(0, EARLY // 2, build_pair, 0)

    for k in range(CAP):
        recv[me * CAP + k] = wave_ref[req_smem[0, me * CAP + k]]
    for d in range(1, count):
        ask(d).wait()
    here = pltpu.make_async_copy(req_all, req_here, local_sem)
    here.start()
    here.wait()

    def data(d, owner):
        return pltpu.make_async_remote_copy(
            src_ref=send.at[d],
            dst_ref=recv.at[pl.ds(owner * CAP, CAP)],
            send_sem=data_send.at[d],
            recv_sem=data_recv.at[d],
            device_id={"tmpl": peer(d)},
            device_id_type=MESH,
        )

    for d in range(1, count):
        back = (4 - d // 4) % 4 * 4 + (4 - d % 4) % 4
        for k in range(CAP):
            send[d, k] = wave_ref[req_here[back, 0, me * CAP + k]]
        data(d, me).start()

    lax.fori_loop(EARLY // 2, slots // 2, build_pair, 0)

    column = lax.broadcasted_iota(jnp.int32, (DEPTH, LANES), 0)
    lagged = lax.broadcasted_iota(jnp.int32, (DEPTH, LANES), 1)
    band[...] = jnp.where((column >= lagged) & (column < lagged + TAPS), 1.0, 0.0).astype(jnp.bfloat16)
    wave32[:, ROWS:, :] = jnp.zeros((wave32.shape[0], wave32.shape[1] - ROWS, LANES), jnp.float32)

    def energies(c):
        for p in range(4):
            wave32[c + p, :BLOCKS, :] = recv[c + p].astype(jnp.float32)
            for a in range(SPAN):
                width = min(LANES, DEPTH - a * LANES)
                frame = wave32[c + p, a : a + ROWS, :width].astype(jnp.bfloat16)
                squares[p * ROWS : (p + 1) * ROWS, a * LANES : a * LANES + width] = frame * frame
        energy = jnp.dot(squares[...], band[...], preferred_element_type=jnp.float32)
        energy = lax.rsqrt(energy + EPS)
        for p in range(4):
            inv[c + p] = energy[p * ROWS : (p + 1) * ROWS, :]

    def arrive(d, carry):
        owner = source(d)

        @pl.when(d > 0)
        def _():
            data(d, owner).wait_recv()

        energies(owner * CAP)
        energies(owner * CAP + 4)
        return carry

    lax.fori_loop(0, count, arrive, 0)

    edge = lax.broadcasted_iota(jnp.int32, (LAG_BLOCKS, LANES), 1)

    def apply(s, rolled):
        row = row_ref[s]
        move = move_ref[s]
        coarse = move // LANES
        fine = move % LANES
        frame = jnp.concatenate(
            [wave32[row, a : a + ROWS, : min(LANES, DEPTH - a * LANES)] for a in range(SPAN)], axis=1
        ).astype(jnp.bfloat16)
        corr = jnp.dot(frame, toep[s], preferred_element_type=jnp.float32)
        normed = corr * jnp.broadcast_to(norm[pl.ds(s, 1), :], corr.shape) * inv[row]
        normed = normed.astype(jnp.bfloat16).astype(jnp.float32)
        rolled[...] = pltpu.roll(normed, (LANES - fine) % LANES, 1)
        near_rows = rolled[pl.ds(coarse, LAG_BLOCKS), :]
        far_rows = rolled[pl.ds(coarse + 1, LAG_BLOCKS), :]
        ncc[pl.ds(s * PITCH, LAG_BLOCKS), :] = jnp.where(edge < LANES - fine, near_rows, far_rows)

    def apply_group(i, carry):
        for p, rolled in enumerate((roll0, roll1, roll2, roll3)):
            apply(4 * i + p, rolled)
        return carry

    lax.fori_loop(0, slots // 4, apply_group, 0)

    names = lax.broadcasted_iota(jnp.int32, (TPL_DEV, slots), 0)
    label[...] = jnp.where(names == jnp.broadcast_to(tmpl_ref[...], (TPL_DEV, slots)), 1.0, 0.0).astype(jnp.bfloat16)

    def block(other, side, q):
        at = (other * 2 + (core + side) % 2) * 8 + q
        picked = ncc[pl.ds(at, slots, stride=PITCH), :].astype(jnp.bfloat16)
        return jnp.dot(label[...], picked, preferred_element_type=jnp.float32)

    others = [(z + step) % 4 for step in steps] + [z]
    firsts = []
    for n, other in enumerate(others):
        for q in range(8):
            near_out[n, q] = block(other, 1, q).astype(jnp.bfloat16)
        copy = pltpu.make_async_remote_copy(
            src_ref=near_out.at[n],
            dst_ref=near.at[n],
            send_sem=near_send.at[n],
            recv_sem=near_recv.at[n],
            device_id={"sta": partner},
            device_id_type=MESH,
        )
        copy.start()
        firsts.append(copy)
    seconds = []
    for n, other in enumerate(others):
        for q in range(8):
            keep[q] = block(other, 0, q)
        firsts[n].wait_recv()
        if n == 3:
            break
        for q in range(8):
            far_out[n, q] = (keep[q] + near[n, q].astype(jnp.float32)).astype(jnp.bfloat16)
        copy = pltpu.make_async_remote_copy(
            src_ref=far_out.at[n],
            dst_ref=far.at[n],
            send_sem=far_send.at[n],
            recv_sem=far_recv.at[n],
            device_id={"sta": other * 2 + core},
            device_id_type=MESH,
        )
        copy.start()
        seconds.append(copy)
    for q in range(8):
        keep[q] = keep[q] + near[3, q].astype(jnp.float32)
    for d in range(1, count):
        data(d, me).wait_send()
    for copy in firsts:
        copy.wait_send()
    for copy in seconds:
        copy.wait()
    for q in range(8):
        total = keep[q]
        for n in range(3):
            total = total + far[n, q].astype(jnp.float32)
        out_ref[q * LANES : (q + 1) * LANES, :] = total.T


def stack_all(request, rows, moveouts, waves, taps, templates):
    slots = taps.shape[0]
    owners = lax.axis_size("tmpl")
    channels = owners * CAP
    waves = waves.reshape(waves.shape[0], BLOCKS, LANES)
    wide = jnp.broadcast_to(request[None, :], (8, channels))
    vmem = pl.BlockSpec(memory_space=pltpu.VMEM)
    smem = pl.BlockSpec(memory_space=pltpu.SMEM)
    f32, bf16 = jnp.float32, jnp.bfloat16
    dma = pltpu.SemaphoreType.DMA
    return pl.pallas_call(
        stack_kernel,
        out_shape=jax.ShapeDtypeStruct((8 * LANES, TPL_DEV), f32),
        in_specs=[smem, smem, smem, vmem, vmem, vmem, vmem],
        out_specs=vmem,
        scratch_shapes=[
            pltpu.VMEM((owners, 8, LANES), jnp.int32),
            pltpu.VMEM((owners, CAP, BLOCKS, LANES), bf16),
            pltpu.VMEM((channels, BLOCKS, LANES), bf16),
            pltpu.VMEM((channels, ROWS + 8, LANES), f32),
            pltpu.VMEM((channels, ROWS, LANES), f32),
            pltpu.VMEM((DEPTH, LANES), bf16),
            pltpu.VMEM((4, slots, LANES), f32),
            pltpu.VMEM((slots, LANES), f32),
            pltpu.VMEM((slots, DEPTH, LANES), bf16),
            pltpu.VMEM((4 * ROWS, DEPTH), bf16),
            pltpu.VMEM((ROWS, LANES), f32),
            pltpu.VMEM((ROWS, LANES), f32),
            pltpu.VMEM((ROWS, LANES), f32),
            pltpu.VMEM((ROWS, LANES), f32),
            pltpu.VMEM((slots * PITCH, LANES), f32),
            pltpu.VMEM((TPL_DEV, slots), bf16),
            pltpu.VMEM((4, 8, TPL_DEV, LANES), bf16),
            pltpu.VMEM((4, 8, TPL_DEV, LANES), bf16),
            pltpu.VMEM((3, 8, TPL_DEV, LANES), bf16),
            pltpu.VMEM((3, 8, TPL_DEV, LANES), bf16),
            pltpu.VMEM((8, TPL_DEV, LANES), f32),
            pltpu.SMEM((owners, 8, LANES), jnp.int32),
            dma((owners,)),
            dma((owners,)),
            dma((owners,)),
            dma((owners,)),
            dma((4,)),
            dma((4,)),
            dma((3,)),
            dma((3,)),
            dma,
        ],
        compiler_params=pltpu.CompilerParams(collective_id=0, has_side_effects=True, vmem_limit_bytes=67043328),
        name="stack",
    )(wide, rows, moveouts, wide, waves, taps, templates[None, :])


def per_device(waveforms, template_taps, slot_template, slot_channel, slot_moveout):
    groups = lax.axis_size("sta")
    owners = lax.axis_size("tmpl")
    request, rows = plan_rows(slot_channel, waveforms.shape[0], owners, groups)
    return stack_all(request, rows, slot_moveout, waveforms, template_taps, slot_template)


def solution(mesh):
    return jax.shard_map(
        per_device,
        mesh=mesh,
        in_specs=(
            P(("tmpl", "sta"), None),
            P(("tmpl", "sta"), None),
            P(("tmpl", "sta")),
            P(("tmpl", "sta")),
            P(("tmpl", "sta")),
        ),
        out_specs=P("sta", "tmpl"),
        check_vma=False,
    )
```

time: 553 us -> 93 us (0.17)
  local copies, waits for them, and re-layouts: 266 us -> 5.89 us
  waiting for transfers between devices: 136 us -> 0 us
  matrix products: 124 us -> 0 us
  Pallas kernels: 0 us -> 86.2 us
  between operations: 13.4 us -> 0.03 us
  other arithmetic: 8.36 us -> 0.6 us
    dot_general x24 -> x0, matrix products: 124 us -> none  [the longest x6 48.6 us: one_block(): jnp.einsum('bk,bku->bu', tap_rows, placer, preferred_element_type=jnp.flo...]
    all_gather x1 -> x0, waiting for transfers between devices: 99.6 us -> none  [per_device(): source_rows = lax.all_gather(waveforms, 'tmpl', axis=0, tiled=True)]
    another operation x12 -> x0, local copies, waits for them, and re-layouts: 94.7 us -> none  [toeplitz(): tiled = jnp.tile(padded, (1, 128))[:, :128 * span_width]]
    pallas_call x0 -> x1, Pallas kernels: none -> 86.2 us  [stack_all(): pl.pallas_call(stack_kernel, out_shape=jax.ShapeDtypeStruct((8 * LANES, T...]
    gather x12 -> x0, local copies, waits for them, and re-layouts: 66.6 us -> none  [one_block(): segment = table[block_index]]
    while x66 -> x0, local copies, waits for them, and re-layouts: 45.2 us -> none
    reduce_scatter x1 -> x0, waiting for transfers between devices: 35.3 us -> none  [per_device(): return lax.psum_scatter(stack, 'sta', scatter_dimension=0, tiled=True)]
    reshape x3 -> x1, local copies, waits for them, and re-layouts: 29.1 us -> 2.32 us  [stack_all(): waves = waves.reshape(waves.shape[0], BLOCKS, LANES)]
  transfers between devices with their start and end apart: 2 -> 0, of which waited for: 2 -> 0; matrix products, arithmetic and copies ran while one was open for 0% -> 0% of each run, Pallas kernels for 0% -> 0%
where the time goes in v2:
time: 93 us; the launch traced here: 92.7 us
  Pallas kernels  86.2 us (93%)
  local copies, waits for them, and re-layouts  5.89 us (6%)
    pallas_call x1, Pallas kernels, stack_all(): pl.pallas_call(stack_kernel, out_shape=jax.ShapeDtypeStruct((8 * LANES, T...  86.2 us
    unnamed x5, local copies, waits for them, and re-layouts  2.98 us
    reshape x1, local copies, waits for them, and re-layouts, stack_all(): waves = waves.reshape(waves.shape[0], BLOCKS, LANES)  2.32 us

profile of v2, /device:TPU:1, one launch (start us, length us, event | category | flops | bytes accessed | tf_op | source)
XLA Modules:
  0.0 92.7 jit_solution(4437997579490784384)
XLA Ops:
  0.0 0.0 copy-start.1
  0.0 0.7 copy-done.1
  0.7 0.2 fusion.1
  0.9 0.2 convert_reduce_fusion
  1.1 0.0 copy-start
  1.1 0.2 select_reduce_fusion
  1.3 0.4 copy-done
  1.7 0.6 broadcast_in_dim.14.req_smem.req_ref
  2.3 2.3 %reshape.16.wave_ref = bf16[48,71,128]{2,1,0:T(8,128)(2,1)} reshape(bf16[48,9088]{1,0:T(8,128)(2,1)} %param.5) | data formatting | bytes 1744896 | tf_op jit(solution)/shard_map/reshape | solution.py:258
  4.6 86.2 %stack.1 = f32[1024,128]{1,0:T(8,128)} custom-call(s32[8,128]{1,0:T(8,128)} %broadcast_in_dim.14.req_smem.req_ref, s32[192]{0:T(256)} %copy-done, s32[192]{0:T(256)} %move_ref.1, s32[8,128]{1,0:T(8,128)} %broadcast_in_dim.14.req_smem.req_ref, bf16[48,71,128]{2,1,0:T(8,128)(2,1)} %reshape.16.wave_ref, bf16[192,400]{1,0:T(8,128)(2,1)} %taps_ref.1, ...), custom_call_target="tpu_custom_call" | custom-call | tf_op jit(solution)/shard_map/stack/pallas_call | solution.py:264
  90.9 1.9 %copy.7 = f32[1024,128]{1,0:T(8,128)} copy(f32[1024,128]{1,0:T(8,128)} %stack.1) | data formatting | bytes 1048576
  (3 shorter events, 0.0 us)
Async XLA Ops:
  0.0 0.7 copy-start.1
  1.1 0.6 copy-start

commit v3 on v2

--- a/solution.py
+++ b/solution.py
@@ -17,12 +17,15 @@
 SCALE = math.sqrt(TAPS / CH_TPL)
 LANES = 128
 SPAN = 5
-DEPTH = 528
+HALF = 256
+DEPTH = HALF + 16
 LAG_BLOCKS = LAGS // LANES
 BLOCKS = 71
 ROWS = 72
 PITCH = LAG_BLOCKS + 1
 EARLY = 32
+GROUP = 8
+BUILD = 2
 MESH = pl.DeviceIdType.MESH
 
 
@@ -43,7 +46,7 @@
 
 def stack_kernel(
     req_smem, row_ref, move_ref, req_ref, wave_ref, taps_ref, tmpl_ref, out_ref,
-    req_all, send, recv, wave32, inv, band, flipped, norm, toep, squares, roll0, roll1, roll2, roll3, ncc, label,
+    req_all, send, recv, wave32, inv, band, flipped, norm, toep, squares, lows, head, tail, rolls, ncc, label,
     near_out, near, far_out, far, keep, req_here,
     req_send, req_recv, data_send, data_recv, near_send, near_recv, far_send, far_recv, local_sem,
 ):
@@ -94,24 +97,27 @@
     for d in range(1, count):
         ask(d).start()
 
-    lower = lane <= sub
+    lower = lax.broadcasted_iota(jnp.int16, (LANES, LANES), 1) <= lax.broadcasted_iota(jnp.int16, (LANES, LANES), 0)
 
     def build(s):
-        last = jnp.zeros((LANES, LANES), jnp.float32)
+        last = jnp.zeros((LANES, LANES), jnp.bfloat16)
         for b in range(4):
-            circ = jnp.broadcast_to(flipped[b, pl.ds(s, 1), :], (LANES, LANES))
-            circ = pltpu.roll(circ, 0, 1, stride=1, stride_axis=0)
-            toep[s, b * LANES : (b + 1) * LANES, :] = jnp.where(lower, circ, last).astype(jnp.bfloat16)
+            base = jnp.broadcast_to(flipped[b, pl.ds(s, 1), :], (16, LANES))
+            base = pltpu.roll(base, 0, 1, stride=1, stride_axis=0).astype(jnp.bfloat16)
+            circ = jnp.concatenate([base if g == 0 else pltpu.roll(base, 16 * g, 1) for g in range(8)], axis=0)
+            down, across = b % 2 * LANES, b // 2 * LANES
+            toep[s, down : down + LANES, across : across + LANES] = jnp.where(lower, circ, last)
             last = circ
-        tail = DEPTH - 4 * LANES
-        toep[s, 4 * LANES :, :] = jnp.where(lower[:tail], 0.0, last[:tail]).astype(jnp.bfloat16)
+        tail = DEPTH - HALF
+        toep[s, HALF:, :LANES] = jnp.where(lower[:tail], jnp.zeros((tail, LANES), jnp.bfloat16), last[:tail])
+        toep[s, HALF:, LANES:] = jnp.zeros((tail, LANES), jnp.bfloat16)
 
     def build_pair(i, carry):
-        build(2 * i)
-        build(2 * i + 1)
+        for p in range(BUILD):
+            build(BUILD * i + p)
         return carry
 
-    lax.fori_loop(0, EARLY // 2, build_pair, 0)
+    lax.fori_loop(0, EARLY // BUILD, build_pair, 0)
 
     for k in range(CAP):
         recv[me * CAP + k] = wave_ref[req_smem[0, me * CAP + k]]
@@ -137,24 +143,27 @@
             send[d, k] = wave_ref[req_here[back, 0, me * CAP + k]]
         data(d, me).start()
 
-    lax.fori_loop(EARLY // 2, slots // 2, build_pair, 0)
-
-    column = lax.broadcasted_iota(jnp.int32, (DEPTH, LANES), 0)
-    lagged = lax.broadcasted_iota(jnp.int32, (DEPTH, LANES), 1)
+    lax.fori_loop(EARLY // BUILD, slots // BUILD, build_pair, 0)
+
+    column = lax.broadcasted_iota(jnp.int32, (DEPTH, HALF), 0)
+    across = lax.broadcasted_iota(jnp.int32, (DEPTH, HALF), 1)
+    column = jnp.where(column < HALF, column + across // LANES * HALF, column + HALF + across // LANES * HALF)
+    lagged = across % LANES
     band[...] = jnp.where((column >= lagged) & (column < lagged + TAPS), 1.0, 0.0).astype(jnp.bfloat16)
     wave32[:, ROWS:, :] = jnp.zeros((wave32.shape[0], wave32.shape[1] - ROWS, LANES), jnp.float32)
 
-    def energies(c):
+    parts = ((0, 0, LANES), (1, LANES, LANES), (4, HALF, DEPTH - HALF))
+
+    def energies(c, squares, lows):
         for p in range(4):
             wave32[c + p, :BLOCKS, :] = recv[c + p].astype(jnp.float32)
-            for a in range(SPAN):
-                width = min(LANES, DEPTH - a * LANES)
+            for a, at, width in parts:
                 frame = wave32[c + p, a : a + ROWS, :width].astype(jnp.bfloat16)
-                squares[p * ROWS : (p + 1) * ROWS, a * LANES : a * LANES + width] = frame * frame
+                squares[p * ROWS : (p + 1) * ROWS, at : at + width] = frame * frame
         energy = jnp.dot(squares[...], band[...], preferred_element_type=jnp.float32)
-        energy = lax.rsqrt(energy + EPS)
+        lows[...] = energy[:, LANES:]
         for p in range(4):
-            inv[c + p] = energy[p * ROWS : (p + 1) * ROWS, :]
+            inv[c + p, : ROWS - 2] = lax.rsqrt(energy[p * ROWS : (p + 1) * ROWS - 2, :LANES] + lows[p * ROWS + 2 : (p + 1) * ROWS, :] + EPS)
 
     def arrive(d, carry):
         owner = source(d)
@@ -163,50 +172,68 @@
         def _():
             data(d, owner).wait_recv()
 
-        energies(owner * CAP)
-        energies(owner * CAP + 4)
+        for h in range(2):
+            energies(owner * CAP + 4 * h, squares[h], lows[h])
         return carry
 
     lax.fori_loop(0, count, arrive, 0)
 
     edge = lax.broadcasted_iota(jnp.int32, (LAG_BLOCKS, LANES), 1)
 
-    def apply(s, rolled):
+    def product(s, p):
+        row = row_ref[s]
+        frame = jnp.concatenate([wave32[row, a : a + ROWS, :width] for a, at, width in parts], axis=1).astype(jnp.bfloat16)
+        corr = jnp.dot(frame, toep[s], preferred_element_type=jnp.float32)
+        head[p][...] = corr[:, :LANES]
+        tail[p][:ROWS, :] = corr[:, LANES:]
+
+    def settle(s, p):
         row = row_ref[s]
         move = move_ref[s]
         coarse = move // LANES
         fine = move % LANES
-        frame = jnp.concatenate(
-            [wave32[row, a : a + ROWS, : min(LANES, DEPTH - a * LANES)] for a in range(SPAN)], axis=1
-        ).astype(jnp.bfloat16)
-        corr = jnp.dot(frame, toep[s], preferred_element_type=jnp.float32)
+        corr = head[p][...] + tail[p][2 : ROWS + 2, :]
         normed = corr * jnp.broadcast_to(norm[pl.ds(s, 1), :], corr.shape) * inv[row]
         normed = normed.astype(jnp.bfloat16).astype(jnp.float32)
+        rolled = rolls[p]
         rolled[...] = pltpu.roll(normed, (LANES - fine) % LANES, 1)
         near_rows = rolled[pl.ds(coarse, LAG_BLOCKS), :]
         far_rows = rolled[pl.ds(coarse + 1, LAG_BLOCKS), :]
         ncc[pl.ds(s * PITCH, LAG_BLOCKS), :] = jnp.where(edge < LANES - fine, near_rows, far_rows)
 
+    for p in range(GROUP):
+        product(p, p)
+
     def apply_group(i, carry):
-        for p, rolled in enumerate((roll0, roll1, roll2, roll3)):
-            apply(4 * i + p, rolled)
+        for p in range(GROUP):
+            settle(GROUP * (i - 1) + p, p)
+        for p in range(GROUP):
+            product(GROUP * i + p, p)
         return carry
 
-    lax.fori_loop(0, slots // 4, apply_group, 0)
+    lax.fori_loop(1, slots // GROUP, apply_group, 0)
+    for p in range(GROUP):
+        settle(slots - GROUP + p, p)
 
     names = lax.broadcasted_iota(jnp.int32, (TPL_DEV, slots), 0)
     label[...] = jnp.where(names == jnp.broadcast_to(tmpl_ref[...], (TPL_DEV, slots)), 1.0, 0.0).astype(jnp.bfloat16)
 
     def block(other, side, q):
-        at = (other * 2 + (core + side) % 2) * 8 + q
-        picked = ncc[pl.ds(at, slots, stride=PITCH), :].astype(jnp.bfloat16)
+        at = (other * 2 + (core + side) % 2) * 8 + 2 * q
+        picked = jnp.concatenate([ncc[pl.ds(at + e, slots, stride=PITCH), :] for e in range(2)], axis=1).astype(jnp.bfloat16)
         return jnp.dot(label[...], picked, preferred_element_type=jnp.float32)
 
     others = [(z + step) % 4 for step in steps] + [z]
     firsts = []
     for n, other in enumerate(others):
-        for q in range(8):
-            near_out[n, q] = block(other, 1, q).astype(jnp.bfloat16)
+
+        def outside(q, carry):
+            total = block(other, 1, q).astype(jnp.bfloat16)
+            near_out[n, 2 * q] = total[:, :LANES]
+            near_out[n, 2 * q + 1] = total[:, LANES:]
+            return carry
+
+        lax.fori_loop(0, 4, outside, 0)
         copy = pltpu.make_async_remote_copy(
             src_ref=near_out.at[n],
             dst_ref=near.at[n],
@@ -219,13 +246,21 @@
         firsts.append(copy)
     seconds = []
     for n, other in enumerate(others):
-        for q in range(8):
-            keep[q] = block(other, 0, q)
         firsts[n].wait_recv()
+
+        def inside(q, carry):
+            total = block(other, 0, q)
+            for e in range(2):
+                summed = total[:, e * LANES : (e + 1) * LANES] + near[n, 2 * q + e].astype(jnp.float32)
+                if n == 3:
+                    keep[2 * q + e] = summed
+                else:
+                    far_out[n, 2 * q + e] = summed.astype(jnp.bfloat16)
+            return carry
+
+        lax.fori_loop(0, 4, inside, 0)
         if n == 3:
             break
-        for q in range(8):
-            far_out[n, q] = (keep[q] + near[n, q].astype(jnp.float32)).astype(jnp.bfloat16)
         copy = pltpu.make_async_remote_copy(
             src_ref=far_out.at[n],
             dst_ref=far.at[n],
@@ -236,8 +271,6 @@
         )
         copy.start()
         seconds.append(copy)
-    for q in range(8):
-        keep[q] = keep[q] + near[3, q].astype(jnp.float32)
     for d in range(1, count):
         data(d, me).wait_send()
     for copy in firsts:
@@ -272,15 +305,15 @@
             pltpu.VMEM((channels, BLOCKS, LANES), bf16),
             pltpu.VMEM((channels, ROWS + 8, LANES), f32),
             pltpu.VMEM((channels, ROWS, LANES), f32),
-            pltpu.VMEM((DEPTH, LANES), bf16),
+            pltpu.VMEM((DEPTH, HALF), bf16),
             pltpu.VMEM((4, slots, LANES), f32),
             pltpu.VMEM((slots, LANES), f32),
-            pltpu.VMEM((slots, DEPTH, LANES), bf16),
-            pltpu.VMEM((4 * ROWS, DEPTH), bf16),
-            pltpu.VMEM((ROWS, LANES), f32),
-            pltpu.VMEM((ROWS, LANES), f32),
-            pltpu.VMEM((ROWS, LANES), f32),
-            pltpu.VMEM((ROWS, LANES), f32),
+            pltpu.VMEM((slots, DEPTH, HALF), bf16),
+            [pltpu.VMEM((4 * ROWS, DEPTH), bf16)] * 2,
+            [pltpu.VMEM((4 * ROWS, LANES), f32)] * 2,
+            [pltpu.VMEM((ROWS, LANES), f32)] * GROUP,
+            [pltpu.VMEM((ROWS + 8, LANES), f32)] * GROUP,
+            [pltpu.VMEM((ROWS, LANES), f32)] * GROUP,
             pltpu.VMEM((slots * PITCH, LANES), f32),
             pltpu.VMEM((TPL_DEV, slots), bf16),
             pltpu.VMEM((4, 8, TPL_DEV, LANES), bf16),

time: 93 us -> 86 us (0.925)
  Pallas kernels: 86.2 us -> 79.2 us
    pallas_call x1, Pallas kernels: 86.2 us -> 79.2 us  [stack_all(): pl.pallas_call(stack_kernel, out_shape=jax.ShapeDtypeStruct((8 * LANES, T...]
where the time goes in v3:
time: 86 us; the launch traced here: 85.8 us
  Pallas kernels  79.2 us (92%)
  local copies, waits for them, and re-layouts  5.89 us (7%)
    pallas_call x1, Pallas kernels, stack_all(): pl.pallas_call(stack_kernel, out_shape=jax.ShapeDtypeStruct((8 * LANES, T...  79.2 us
    unnamed x5, local copies, waits for them, and re-layouts  2.98 us
    reshape x1, local copies, waits for them, and re-layouts, stack_all(): waves = waves.reshape(waves.shape[0], BLOCKS, LANES)  2.32 us

profile of v3, /device:TPU:1, one launch (start us, length us, event | category | flops | bytes accessed | tf_op | source)
XLA Modules:
  0.0 85.8 jit_solution(8332282232214103106)
XLA Ops:
  0.0 0.0 copy-start.1
  0.0 0.7 copy-done.1
  0.7 0.2 fusion.1
  0.9 0.2 convert_reduce_fusion
  1.1 0.0 copy-start
  1.1 0.2 select_reduce_fusion
  1.3 0.4 copy-done
  1.7 0.6 broadcast_in_dim.14.req_smem.req_ref
  2.3 2.3 %reshape.16.wave_ref = bf16[48,71,128]{2,1,0:T(8,128)(2,1)} reshape(bf16[48,9088]{1,0:T(8,128)(2,1)} %param.5) | data formatting | bytes 1744896 | tf_op jit(solution)/shard_map/reshape | solution.py:291
  4.6 79.2 %stack.1 = f32[1024,128]{1,0:T(8,128)} custom-call(s32[8,128]{1,0:T(8,128)} %broadcast_in_dim.14.req_smem.req_ref, s32[192]{0:T(256)} %copy-done, s32[192]{0:T(256)} %move_ref.1, s32[8,128]{1,0:T(8,128)} %broadcast_in_dim.14.req_smem.req_ref, bf16[48,71,128]{2,1,0:T(8,128)(2,1)} %reshape.16.wave_ref, bf16[192,400]{1,0:T(8,128)(2,1)} %taps_ref.1, ...), custom_call_target="tpu_custom_call" | custom-call | tf_op jit(solution)/shard_map/stack/pallas_call | solution.py:297
  83.9 1.9 %copy.7 = f32[1024,128]{1,0:T(8,128)} copy(f32[1024,128]{1,0:T(8,128)} %stack.1) | data formatting | bytes 1048576
  (3 shorter events, 0.0 us)
Async XLA Ops:
  0.0 0.7 copy-start.1
  1.1 0.6 copy-start

commit v4 on v3

v4 whole, which is shorter than its diff:
```python
import functools
import math

import jax
import jax.numpy as jnp
from jax import lax
from jax.experimental import pallas as pl
from jax.experimental.pallas import tpu as pltpu
from jax.sharding import PartitionSpec as P

TAPS = 400
CH_TPL = 30
LAGS = 8192
TPL_DEV = 128
CAP = 8
EPS = 1e-06
SCALE = math.sqrt(TAPS / CH_TPL)
LANES = 128
SPAN = 5
HALF = 256
DEPTH = HALF + 16
LAG_BLOCKS = LAGS // LANES
BLOCKS = 71
ROWS = 72
CHUNK = 16
PITCH = CHUNK + 1
WINDOW = 24
PARTS = (0, 32, 48, 64, 72)
EARLY = 32
GROUP = 8
BUILD = 2
MESH = pl.DeviceIdType.MESH


def plan_rows(slot_channel, channels_here, owners, groups):
    owner = slot_channel // channels_here // groups
    local = slot_channel % channels_here
    key = owner * channels_here + local
    count = key.shape[0]
    order = jnp.arange(count, dtype=jnp.int32)
    earlier = (key[:, None] == key[None, :]) & (order[None, :] < order[:, None])
    first = ~jnp.any(earlier, axis=1)
    below = (owner[:, None] == owner[None, :]) & (key[None, :] < key[:, None]) & first[None, :]
    row = owner * CAP + jnp.sum(below.astype(jnp.int32), axis=1)
    hit = (row[:, None] == jnp.arange(owners * CAP, dtype=jnp.int32)[None, :]) & first[:, None]
    request = jnp.sum(jnp.where(hit, local[:, None], 0), axis=0)
    return request, row


def stack_kernel(
    req_smem, row_ref, move_ref, req_ref, wave_ref, taps_ref, tmpl_ref, out_ref,
    req_all, turned, send, recv, wave32, inv, band, flipped, norm, toep, squares, lows, head, tail, rolls, ncc, label,
    near_out, near, far_out, far, keep, req_here,
    req_send, req_recv, data_send, data_recv, near_send, near_recv, far_send, far_recv, local_sem,
):
    slots = taps_ref.shape[0]
    me = lax.axis_index("tmpl")
    x, y = me // 4, me % 4
    group = lax.axis_index("sta")
    z, core = group // 2, group % 2
    partner = z * 2 + (core + 1) % 2
    steps = (2, 1, 3)
    count = 16

    def peer(d):
        return ((x + d // 4) % 4) * 4 + (y + d % 4) % 4

    def source(d):
        return ((x + 4 - d // 4) % 4) * 4 + (y + 4 - d % 4) % 4

    barrier = pltpu.get_barrier_semaphore()
    for d in range(1, count):
        pl.semaphore_signal(barrier, inc=1, device_id={"tmpl": peer(d)}, device_id_type=MESH)
    for other in [partner] + [((z + step) % 4) * 2 + core for step in steps]:
        pl.semaphore_signal(barrier, inc=1, device_id={"sta": other}, device_id_type=MESH)

    sub = lax.broadcasted_iota(jnp.int32, (LANES, LANES), 0)
    lane = lax.broadcasted_iota(jnp.int32, (LANES, LANES), 1)
    flip = jnp.where(sub == (LANES - lane) % LANES, 1.0, 0.0).astype(jnp.bfloat16)
    power = jnp.zeros((slots, 1), jnp.float32)
    for b in range(4):
        piece = taps_ref[:, b * LANES : min(b * LANES + LANES, TAPS)]
        wide = piece.shape[1]
        flipped[b] = jnp.dot(piece, flip[:wide, :], preferred_element_type=jnp.float32)
        piece = piece.astype(jnp.float32)
        power = power + jnp.sum(piece * piece, axis=1, keepdims=True)
    norm[...] = jnp.broadcast_to(SCALE * lax.rsqrt(power + EPS), (slots, LANES))
    lead = (z + 1) % 4
    turns = []
    for i in range(9):
        turn = 2 * lead + i
        turns.append(pl.multiple_of(jnp.where(turn >= 9, turn - 9, turn) * 8, 8))

    def rotate(c, carry):
        for i in range(9):
            turned[c, 8 * i : 8 * i + 8, :] = wave_ref[c, pl.ds(turns[i], 8), :]
        return carry

    lax.fori_loop(0, turned.shape[0], rotate, 0)
    pl.semaphore_wait(barrier, count - 1 + 4)

    def ask(d):
        return pltpu.make_async_remote_copy(
            src_ref=req_ref,
            dst_ref=req_all.at[d],
            send_sem=req_send.at[d],
            recv_sem=req_recv.at[d],
            device_id={"tmpl": peer(d)},
            device_id_type=MESH,
        )

    for d in range(1, count):
        ask(d).start()

    lower = lax.broadcasted_iota(jnp.int16, (LANES, LANES), 1) <= lax.broadcasted_iota(jnp.int16, (LANES, LANES), 0)

    def build(s):
        last = jnp.zeros((LANES, LANES), jnp.bfloat16)
        for b in range(4):
            base = jnp.broadcast_to(flipped[b, pl.ds(s, 1), :], (16, LANES))
            base = pltpu.roll(base, 0, 1, stride=1, stride_axis=0).astype(jnp.bfloat16)
            circ = jnp.concatenate([base if g == 0 else pltpu.roll(base, 16 * g, 1) for g in range(8)], axis=0)
            down, across = b % 2 * LANES, b // 2 * LANES
            toep[s, down : down + LANES, across : across + LANES] = jnp.where(lower, circ, last)
            last = circ
        tail = DEPTH - HALF
        toep[s, HALF:, :LANES] = jnp.where(lower[:tail], jnp.zeros((tail, LANES), jnp.bfloat16), last[:tail])
        toep[s, HALF:, LANES:] = jnp.zeros((tail, LANES), jnp.bfloat16)

    def build_pair(i, carry):
        for p in range(BUILD):
            build(BUILD * i + p)
        return carry

    lax.fori_loop(0, EARLY // BUILD, build_pair, 0)

    for k in range(CAP):
        recv[me * CAP + k] = turned[req_smem[0, me * CAP + k]]
    for d in range(1, count):
        ask(d).wait()
    here = pltpu.make_async_copy(req_all, req_here, local_sem)
    here.start()
    here.wait()

    def data(d, part, owner):
        rows = pl.ds(PARTS[part], PARTS[part + 1] - PARTS[part])
        return pltpu.make_async_remote_copy(
            src_ref=send.at[d, :, rows],
            dst_ref=recv.at[pl.ds(owner * CAP, CAP), rows],
            send_sem=data_send.at[d, part],
            recv_sem=data_recv.at[d, part],
            device_id={"tmpl": peer(d)},
            device_id_type=MESH,
        )

    for d in range(1, count):
        back = (4 - d // 4) % 4 * 4 + (4 - d % 4) % 4
        for k in range(CAP):
            send[d, k] = turned[req_here[back, 0, me * CAP + k]]
        data(d, 0, me).start()
    for part in range(1, 4):
        for d in range(1, count):
            data(d, part, me).start()

    names = lax.broadcasted_iota(jnp.int32, (TPL_DEV, slots), 0)
    label[...] = jnp.where(names == jnp.broadcast_to(tmpl_ref[...], (TPL_DEV, slots)), 1.0, 0.0).astype(jnp.bfloat16)

    lax.fori_loop(EARLY // BUILD, slots // BUILD, build_pair, 0)

    column = lax.broadcasted_iota(jnp.int32, (DEPTH, HALF), 0)
    across = lax.broadcasted_iota(jnp.int32, (DEPTH, HALF), 1)
    column = jnp.where(column < HALF, column + across // LANES * HALF, column + HALF + across // LANES * HALF)
    lagged = across % LANES
    band[...] = jnp.where((column >= lagged) & (column < lagged + TAPS), 1.0, 0.0).astype(jnp.bfloat16)
    wave32[:, ROWS + 8 :, :] = jnp.zeros((wave32.shape[0], 8, LANES), jnp.float32)
    parts = ((0, 0, LANES), (1, LANES, LANES), (4, HALF, DEPTH - HALF))
    edge = lax.broadcasted_iota(jnp.int32, (CHUNK, LANES), 1)

    def prepare(part, base):
        rows = slice(PARTS[part], PARTS[part + 1])

        def arrive(d, carry):
            data(d, part, source(d)).wait_recv()
            return carry

        lax.fori_loop(1, count, arrive, 0)

        def settle_pair(i, carry):
            for h in range(2):
                c = (2 * i + h) * CAP
                for p in range(CAP):
                    wave32[c + p, rows, :] = recv[c + p, rows, :].astype(jnp.float32)
                    if part == 3:
                        wave32[c + p, ROWS : ROWS + 8, :] = recv[c + p, :8, :].astype(jnp.float32)
            for h in range(2):
                c = (2 * i + h) * CAP
                for p in range(CAP):
                    for a, at, width in parts:
                        frame = wave32[c + p, pl.ds(base + a, WINDOW), :width].astype(jnp.bfloat16)
                        squares[h][p * WINDOW : (p + 1) * WINDOW, at : at + width] = frame * frame
            for h in range(2):
                c = (2 * i + h) * CAP
                energy = jnp.dot(squares[h][...], band[...], preferred_element_type=jnp.float32)
                lows[h][: CAP * WINDOW, :] = energy[:, LANES:]
                energy = energy[:, :LANES] + lows[h][2 : CAP * WINDOW + 2, :]
                energy = lax.rsqrt(energy + EPS)
                for p in range(CAP):
                    inv[c + p] = energy[p * WINDOW : (p + 1) * WINDOW, :]
            return carry

        lax.fori_loop(0, count // 2, settle_pair, 0)

    def correlate(base):
        def product(s, p):
            row = row_ref[s]
            frame = jnp.concatenate(
                [wave32[row, pl.ds(base + a, WINDOW), :width] for a, at, width in parts], axis=1
            ).astype(jnp.bfloat16)
            corr = jnp.dot(frame, toep[s], preferred_element_type=jnp.float32)
            head[p][...] = corr[:, :LANES]
            tail[p][:WINDOW, :] = corr[:, LANES:]

        def settle(s, p):
            row = row_ref[s]
            move = move_ref[s]
            coarse = lax.shift_right_logical(move, 7)
            fine = move & 127
            corr = head[p][...] + tail[p][2 : WINDOW + 2, :]
            normed = corr * jnp.broadcast_to(norm[pl.ds(s, 1), :], corr.shape) * inv[row]
            normed = normed.astype(jnp.bfloat16).astype(jnp.float32)
            rolled = rolls[p]
            rolled[...] = pltpu.roll(normed, (LANES - fine) & 127, 1)
            near_rows = rolled[pl.ds(coarse, CHUNK), :]
            far_rows = rolled[pl.ds(coarse + 1, CHUNK), :]
            ncc[pl.ds(s * PITCH, CHUNK), :] = jnp.where(edge < LANES - fine, near_rows, far_rows)

        for p in range(GROUP):
            product(p, p)

        def apply_group(i, carry):
            for p in range(GROUP):
                settle(GROUP * (i - 1) + p, p)
            for p in range(GROUP):
                product(GROUP * i + p, p)
            return carry

        lax.fori_loop(1, slots // GROUP, apply_group, 0)
        for p in range(GROUP):
            settle(slots - GROUP + p, p)

    def block(side, q):
        at = (core + side) % 2 * 8 + 2 * q
        picked = jnp.concatenate([ncc[pl.ds(at + e, slots, stride=PITCH), :] for e in range(2)], axis=1).astype(jnp.bfloat16)
        return jnp.dot(label[...], picked, preferred_element_type=jnp.float32)

    def near_copy(j):
        return pltpu.make_async_remote_copy(
            src_ref=near_out.at[j],
            dst_ref=near.at[j],
            send_sem=near_send.at[j],
            recv_sem=near_recv.at[j],
            device_id={"sta": partner},
            device_id_type=MESH,
        )

    def far_copy(j):
        return pltpu.make_async_remote_copy(
            src_ref=far_out.at[j],
            dst_ref=far.at[j],
            send_sem=far_send.at[j],
            recv_sem=far_recv.at[j],
            device_id={"sta": (lead + j) % 4 * 2 + core},
            device_id_type=MESH,
        )

    def gather(j):
        def outside(q, carry):
            total = block(1, q).astype(jnp.bfloat16)
            near_out[j, 2 * q] = total[:, :LANES]
            near_out[j, 2 * q + 1] = total[:, LANES:]
            return carry

        lax.fori_loop(0, 4, outside, 0)
        near_copy(j).start()

        def inside(q, carry):
            total = block(0, q)
            keep[j, 2 * q] = total[:, :LANES]
            keep[j, 2 * q + 1] = total[:, LANES:]
            return carry

        lax.fori_loop(0, 4, inside, 0)

    def forward(j):
        near_copy(j).wait_recv()
        for q in range(8):
            far_out[j, q] = (keep[j, q] + near[j, q].astype(jnp.float32)).astype(jnp.bfloat16)
        far_copy(j).start()

    for j in range(4):
        base = pl.multiple_of(16 * j + jnp.where(lead + j >= 4, 8, 0), 8)
        prepare(j, base)
        if j > 0:
            forward(j - 1)
        correlate(base)
        gather(j)
    near_copy(3).wait_recv()
    for q in range(8):
        keep[3, q] = keep[3, q] + near[3, q].astype(jnp.float32)
    for part in range(4):
        for d in range(1, count):
            data(d, part, me).wait_send()
        near_copy(part).wait_send()
    for j in range(3):
        far_copy(j).wait()
    for q in range(8):
        total = keep[3, q]
        for j in range(3):
            total = total + far[j, q].astype(jnp.float32)
        out_ref[q * LANES : (q + 1) * LANES, :] = total.T


def stack_all(request, rows, moveouts, waves, taps, templates):
    slots = taps.shape[0]
    owners = lax.axis_size("tmpl")
    channels = owners * CAP
    waves = jnp.pad(waves.reshape(waves.shape[0], BLOCKS, LANES), ((0, 0), (0, ROWS - BLOCKS), (0, 0)))
    wide = jnp.broadcast_to(request[None, :], (8, channels))
    vmem = pl.BlockSpec(memory_space=pltpu.VMEM)
    smem = pl.BlockSpec(memory_space=pltpu.SMEM)
    f32, bf16 = jnp.float32, jnp.bfloat16
    dma = pltpu.SemaphoreType.DMA
    return pl.pallas_call(
        stack_kernel,
        out_shape=jax.ShapeDtypeStruct((8 * LANES, TPL_DEV), f32),
        in_specs=[smem, smem, smem, vmem, vmem, vmem, vmem],
        out_specs=vmem,
        scratch_shapes=[
            pltpu.VMEM((owners, 8, LANES), jnp.int32),
            pltpu.VMEM(waves.shape, bf16),
            pltpu.VMEM((owners, CAP, ROWS, LANES), bf16),
            pltpu.VMEM((channels, ROWS, LANES), bf16),
            pltpu.VMEM((channels, ROWS + 16, LANES), f32),
            pltpu.VMEM((channels, WINDOW, LANES), f32),
            pltpu.VMEM((DEPTH, HALF), bf16),
            pltpu.VMEM((4, slots, LANES), f32),
            pltpu.VMEM((slots, LANES), f32),
            pltpu.VMEM((slots, DEPTH, HALF), bf16),
            [pltpu.VMEM((CAP * WINDOW, DEPTH), bf16)] * 2,
            [pltpu.VMEM((CAP * WINDOW + 8, LANES), f32)] * 2,
            [pltpu.VMEM((WINDOW, LANES), f32)] * GROUP,
            [pltpu.VMEM((WINDOW + 8, LANES), f32)] * GROUP,
            [pltpu.VMEM((WINDOW, LANES), f32)] * GROUP,
            pltpu.VMEM((slots * PITCH, LANES), f32),
            pltpu.VMEM((TPL_DEV, slots), bf16),
            pltpu.VMEM((4, 8, TPL_DEV, LANES), bf16),
            pltpu.VMEM((4, 8, TPL_DEV, LANES), bf16),
            pltpu.VMEM((3, 8, TPL_DEV, LANES), bf16),
            pltpu.VMEM((3, 8, TPL_DEV, LANES), bf16),
            pltpu.VMEM((4, 8, TPL_DEV, LANES), f32),
            pltpu.SMEM((owners, 8, LANES), jnp.int32),
            dma((owners,)),
            dma((owners,)),
            dma((owners, 4)),
            dma((owners, 4)),
            dma((4,)),
            dma((4,)),
            dma((3,)),
            dma((3,)),
            dma,
        ],
        compiler_params=pltpu.CompilerParams(collective_id=0, has_side_effects=True, vmem_limit_bytes=67043328),
        name="stack",
    )(wide, rows, moveouts, wide, waves, taps, templates[None, :])


def per_device(waveforms, template_taps, slot_template, slot_channel, slot_moveout):
    groups = lax.axis_size("sta")
    owners = lax.axis_size("tmpl")
    request, rows = plan_rows(slot_channel, waveforms.shape[0], owners, groups)
    return stack_all(request, rows, slot_moveout, waveforms, template_taps, slot_template)


def solution(mesh):
    return jax.shard_map(
        per_device,
        mesh=mesh,
        in_specs=(
            P(("tmpl", "sta"), None),
            P(("tmpl", "sta"), None),
            P(("tmpl", "sta")),
            P(("tmpl", "sta")),
            P(("tmpl", "sta")),
        ),
        out_specs=P("sta", "tmpl"),
        check_vma=False,
    )
```

time: 86 us -> 92.9 us (1.080)
  Pallas kernels: 79.2 us -> 85.9 us
    pallas_call x1, Pallas kernels: 79.2 us -> 85.9 us  [stack_all(): pl.pallas_call(stack_kernel, out_shape=jax.ShapeDtypeStruct((8 * LANES, T...]
    pad x0 -> x1, local copies, waits for them, and re-layouts: none -> 1 us  [stack_all(): jnp.pad(waves.reshape(waves.shape[0], BLOCKS, LANES), ((0, 0), (0, ROWS -...]
where the time goes in v4:
time: 92.9 us; the launch traced here: 92.7 us
  Pallas kernels  85.9 us (92%)
  local copies, waits for them, and re-layouts  6.18 us (7%)
    pallas_call x1, Pallas kernels, stack_all(): pl.pallas_call(stack_kernel, out_shape=jax.ShapeDtypeStruct((8 * LANES, T...  85.9 us
    unnamed x5, local copies, waits for them, and re-layouts  2.98 us

profile of v4, /device:TPU:1, one launch (start us, length us, event | category | flops | bytes accessed | tf_op | source)
XLA Modules:
  0.0 92.7 jit_solution(2244123000766197803)
XLA Ops:
  0.0 0.0 copy-start.1
  0.0 0.7 copy-done.1
  0.7 0.2 fusion.1
  0.9 0.2 convert_reduce_fusion
  1.1 0.0 copy-start
  1.1 0.2 select_reduce_fusion
  1.3 0.4 copy-done
  1.7 0.6 broadcast_in_dim.14.req_smem.req_ref
  2.3 1.6 %reshape.16 = bf16[48,71,128]{2,1,0:T(8,128)(2,1)S(1)} reshape(bf16[48,9088]{1,0:T(8,128)(2,1)} %param.5) | data formatting | bytes 1744896 | tf_op jit(solution)/shard_map/reshape | solution.py:327
  3.9 1.0 %pad.4.wave_ref = bf16[48,72,128]{2,1,0:T(8,128)(2,1)} pad(bf16[48,71,128]{2,1,0:T(8,128)(2,1)S(1)} %reshape.16, bf16[]{:T(256)} %constant.38.clone.1), padding=0_0x0_1x0_0 | pad | bytes 1757186 | tf_op jit(solution)/shard_map/jit(_pad)/pad | solution.py:327
  4.9 85.9 %stack.1 = f32[1024,128]{1,0:T(8,128)} custom-call(s32[8,128]{1,0:T(8,128)} %broadcast_in_dim.14.req_smem.req_ref, s32[192]{0:T(256)} %copy-done, s32[192]{0:T(256)} %move_ref.1, s32[8,128]{1,0:T(8,128)} %broadcast_in_dim.14.req_smem.req_ref, bf16[48,72,128]{2,1,0:T(8,128)(2,1)} %pad.4.wave_ref, bf16[192,400]{1,0:T(8,128)(2,1)} %taps_ref.1, s32[1,192]{1,0:T(1,128)} %bitcast.1), custom_call_target="tpu_custom_call" | custom-call | tf_op jit(solution)/shard_map/stack/pallas_call | solution.py:333
  90.8 1.9 %copy.7 = f32[1024,128]{1,0:T(8,128)} copy(f32[1024,128]{1,0:T(8,128)} %stack.1) | data formatting | bytes 1048576
  (3 shorter events, 0.0 us)
Async XLA Ops:
  0.0 0.7 copy-start.1
  1.1 0.6 copy-start
